TPU v7x, 32 devices: a whole 2x2x4 slice. The times are simulated.
32 devices in a mesh: dp: 8 (over z, x), ctx: 4 (over y, core).
Axes of the slice: x: 2, y: 2, z: 4, core: 2. Of those that a mesh axis runs over, the one named last changes fastest.
Arguments:
- tokens: bfloat16 [16, 1024, 960], P('dp', 'ctx'), may hold values from -6 to 6
- segment_ids: int32 [16, 1024], P('dp', 'ctx'), may hold values from 0 to 5, as said below
- positions: int32 [16, 1024], P('dp', 'ctx'), may hold values from 0 to 2047, as said below
- norm_attn: float32 [960], replicated, may hold values from 0.25 to 1.75
- w_query: bfloat16 [921600], P(('dp', 'ctx')), may hold values from -0.1875 to 0.1875
- w_key: bfloat16 [307200], P(('dp', 'ctx')), may hold values from -0.1875 to 0.1875
- w_value: bfloat16 [307200], P(('dp', 'ctx')), may hold values from -0.1875 to 0.1875
- w_out: bfloat16 [921600], P(('dp', 'ctx')), may hold values from -0.75 to 0.75
- norm_ffn: float32 [960], replicated, may hold values from 0.25 to 1.75
- w_gate: bfloat16 [2457600], P(('dp', 'ctx')), may hold values from -0.1875 to 0.1875
- w_up: bfloat16 [2457600], P(('dp', 'ctx')), may hold values from -0.1875 to 0.1875
- w_down: bfloat16 [2457600], P(('dp', 'ctx')), may hold values from -0.125 to 0.125
- cotangent: bfloat16 [16, 1024, 960], P('dp', 'ctx'), may hold values from -6 to 6
Outputs:
- output: bfloat16 [16, 1024, 960], P('dp', 'ctx')
- d_tokens: float32 [16, 1024, 960], P('dp', 'ctx')
- d_norm_attn: float32 [960], replicated
- d_w_query: float32 [921600], P(('dp', 'ctx'))
- d_w_key: float32 [307200], P(('dp', 'ctx'))
- d_w_value: float32 [307200], P(('dp', 'ctx'))
- d_w_out: float32 [921600], P(('dp', 'ctx'))
- d_norm_ffn: float32 [960], replicated
- d_w_gate: float32 [2457600], P(('dp', 'ctx'))
- d_w_up: float32 [2457600], P(('dp', 'ctx'))
- d_w_down: float32 [2457600], P(('dp', 'ctx'))
Inputs may be any that keep to these rules, and one draw needn't show every extreme that they name: `segment_ids`: within each sequence the ids start at 0 and never fall. A run of one id is one document: a sequence's first run may be the rest of a longer document and has 102 positions or more, every later run is a document of 204 to 2047 positions, cut at the sequence's end. Within each run of one segment id the positions rise by one from token to token; every run but a sequence's first starts at 0, a sequence's first run starts at most at 1024.
All inputs are finite; a program needn't handle non-finite values.
Results may differ from a plain program's by a relative error of at most 0.02.
Values may be sent and summed in bfloat16 or wider, within the bound.
No kernel may reach another device: no remote copies, remote signals or barrier semaphores. Data moves between devices by JAX's collectives and lax.ppermute only.
A program may use at most 448 MiB of HBM per device.

v0:
```python
import jax
import jax.numpy as jnp
from jax import lax
from jax.sharding import PartitionSpec as P

D = 960
HEADS = 15
KV_HEADS = 5
HEAD_DIM = 64
FF = 2560
MICRO = 2
norm_eps = 1e-05
rope_base = 100000.0
mask_fill = -1000000000.0


def rms_scale(values):
    return lax.rsqrt(jnp.mean(values * values, axis=-1, keepdims=True) + norm_eps)


def norm_back(values, scale, gain, grad):
    gain_grad = jnp.sum(grad * values * scale, axis=0)
    weighted = grad * gain
    inner = jnp.mean(weighted * values, axis=-1, keepdims=True)
    return (scale * weighted - values * (scale * scale * scale) * inner, gain_grad)


def rope_tables(position):
    freqs = rope_base ** (-jnp.arange(0, HEAD_DIM, 2, dtype=jnp.float32) / HEAD_DIM)
    angles = position.astype(jnp.float32)[..., None] * freqs
    angles = jnp.concatenate([angles, angles], axis=-1)
    return (jnp.cos(angles)[..., None, :], jnp.sin(angles)[..., None, :])


def rotate(values, cosine, sine):
    half = values.shape[-1] // 2
    turned = jnp.concatenate([-values[..., half:], values[..., :half]], axis=-1)
    return values * cosine + turned * sine


def rotate_back(grad, cosine, sine):
    half = grad.shape[-1] // 2
    scaled = grad * sine
    return grad * cosine + jnp.concatenate([scaled[..., half:], -scaled[..., :half]], axis=-1)


def product(left, right):
    return jnp.dot(left, right, preferred_element_type=jnp.float32)


def product_left(left, right):
    return lax.dot_general(
        left, right, (((0,), (0,)), ((), ())), preferred_element_type=jnp.float32
    )


def product_right(left, right):
    return lax.dot_general(
        left, right, (((1,), (1,)), ((), ())), preferred_element_type=jnp.float32
    )


def masked_scores(query_groups, key_heads, allowed, score_scale):
    scores = (
        jnp.einsum("sckgd,slkd->skgcl", query_groups, key_heads, preferred_element_type=jnp.float32)
        * score_scale
    )
    return jnp.where(allowed, scores, mask_fill)


def owner_blocks(terms):
    dp_size = lax.axis_size("dp")
    ctx_size = lax.axis_size("ctx")
    return [term.reshape(dp_size, ctx_size, -1) for term in terms]


def reduce_at_end(terms):
    blocks = owner_blocks(terms)
    moved = (
        lax.all_to_all(
            blocks[0].astype(jnp.bfloat16), "ctx", split_axis=1, concat_axis=1, tiled=True
        ).astype(jnp.float32),
        lax.all_to_all(
            blocks[1].astype(jnp.bfloat16), "ctx", split_axis=1, concat_axis=1, tiled=True
        ).astype(jnp.float32),
        lax.all_to_all(
            blocks[2].astype(jnp.bfloat16), "ctx", split_axis=1, concat_axis=1, tiled=True
        ).astype(jnp.float32),
        lax.all_to_all(
            blocks[3].astype(jnp.bfloat16), "ctx", split_axis=1, concat_axis=1, tiled=True
        ).astype(jnp.float32),
        lax.all_to_all(
            blocks[4].astype(jnp.bfloat16), "ctx", split_axis=1, concat_axis=1, tiled=True
        ).astype(jnp.float32),
        lax.all_to_all(
            blocks[5].astype(jnp.bfloat16), "ctx", split_axis=1, concat_axis=1, tiled=True
        ).astype(jnp.float32),
        lax.all_to_all(
            blocks[6].astype(jnp.bfloat16), "ctx", split_axis=1, concat_axis=1, tiled=True
        ).astype(jnp.float32),
    )
    summed = [jnp.sum(piece, axis=1) for piece in moved]
    owned = (
        lax.psum_scatter(
            summed[0].astype(jnp.bfloat16), "dp", scatter_dimension=0, tiled=True
        ).astype(jnp.float32),
        lax.psum_scatter(
            summed[1].astype(jnp.bfloat16), "dp", scatter_dimension=0, tiled=True
        ).astype(jnp.float32),
        lax.psum_scatter(
            summed[2].astype(jnp.bfloat16), "dp", scatter_dimension=0, tiled=True
        ).astype(jnp.float32),
        lax.psum_scatter(
            summed[3].astype(jnp.bfloat16), "dp", scatter_dimension=0, tiled=True
        ).astype(jnp.float32),
        lax.psum_scatter(
            summed[4].astype(jnp.bfloat16), "dp", scatter_dimension=0, tiled=True
        ).astype(jnp.float32),
        lax.psum_scatter(
            summed[5].astype(jnp.bfloat16), "dp", scatter_dimension=0, tiled=True
        ).astype(jnp.float32),
        lax.psum_scatter(
            summed[6].astype(jnp.bfloat16), "dp", scatter_dimension=0, tiled=True
        ).astype(jnp.float32),
    )
    return [piece.reshape(-1) for piece in owned]


def body(
    tokens,
    segment_ids,
    positions,
    norm_attn,
    w_query,
    w_key,
    w_value,
    w_out,
    norm_ffn,
    w_gate,
    w_up,
    w_down,
    cotangent,
):
    seq_local, block_len, width = tokens.shape
    micro_seqs = seq_local // MICRO
    groups = HEADS // KV_HEADS
    attn_width = HEADS * HEAD_DIM
    kv_width = KV_HEADS * HEAD_DIM
    length = block_len * lax.axis_size("ctx")
    rows = micro_seqs * block_len
    score_scale = HEAD_DIM ** (-0.5)
    query_index = lax.axis_index("ctx") * block_len + jnp.arange(block_len, dtype=jnp.int32)
    key_index = jnp.arange(length, dtype=jnp.int32)
    shapes = (
        (D, attn_width),
        (D, kv_width),
        (D, kv_width),
        (attn_width, D),
        (D, FF),
        (D, FF),
        (FF, D),
    )

    def forward_weights():
        flats = (
            lax.all_gather(w_query, ("dp", "ctx"), axis=0, tiled=True),
            lax.all_gather(w_key, ("dp", "ctx"), axis=0, tiled=True),
            lax.all_gather(w_value, ("dp", "ctx"), axis=0, tiled=True),
            lax.all_gather(w_out, ("dp", "ctx"), axis=0, tiled=True),
            lax.all_gather(w_gate, ("dp", "ctx"), axis=0, tiled=True),
            lax.all_gather(w_up, ("dp", "ctx"), axis=0, tiled=True),
            lax.all_gather(w_down, ("dp", "ctx"), axis=0, tiled=True),
        )
        return [flat.reshape(shape) for flat, shape in zip(flats, shapes)]

    def backward_weights():
        flats = (
            lax.all_gather(w_query, ("dp", "ctx"), axis=0, tiled=True),
            lax.all_gather(w_key, ("dp", "ctx"), axis=0, tiled=True),
            lax.all_gather(w_value, ("dp", "ctx"), axis=0, tiled=True),
            lax.all_gather(w_out, ("dp", "ctx"), axis=0, tiled=True),
            lax.all_gather(w_gate, ("dp", "ctx"), axis=0, tiled=True),
            lax.all_gather(w_up, ("dp", "ctx"), axis=0, tiled=True),
            lax.all_gather(w_down, ("dp", "ctx"), axis=0, tiled=True),
        )
        return [flat.reshape(shape) for flat, shape in zip(flats, shapes)]

    grad_totals = [jnp.zeros(shape, jnp.float32) for shape in shapes]
    shard_totals = [
        jnp.zeros(shard.shape, jnp.float32)
        for shard in (w_query, w_key, w_value, w_out, w_gate, w_up, w_down)
    ]
    attn_gain_total = jnp.zeros((D,), jnp.float32)
    ffn_gain_total = jnp.zeros((D,), jnp.float32)
    outputs = []
    input_grads = []
    for micro in range(MICRO):
        lower = micro * micro_seqs
        upper = lower + micro_seqs
        inputs = tokens[lower:upper].astype(jnp.float32).reshape(rows, D)
        segment_part = segment_ids[lower:upper]
        position_part = positions[lower:upper]
        grad_out = cotangent[lower:upper].astype(jnp.float32).reshape(rows, D)
        query_weight, key_weight, value_weight, out_weight, gate_weight, up_weight, down_weight = (
            forward_weights()
        )
        scale_attn = rms_scale(inputs)
        normed_attn = (inputs * scale_attn * norm_attn).astype(jnp.bfloat16)
        cosine, sine = rope_tables(position_part)
        query_rot = rotate(
            product(normed_attn, query_weight).reshape(micro_seqs, block_len, HEADS, HEAD_DIM),
            cosine,
            sine,
        ).astype(jnp.bfloat16)
        key_rot = (
            rotate(
                product(normed_attn, key_weight).reshape(micro_seqs, block_len, KV_HEADS, HEAD_DIM),
                cosine,
                sine,
            )
            .astype(jnp.bfloat16)
            .reshape(micro_seqs, block_len, kv_width)
        )
        value_low = (
            product(normed_attn, value_weight)
            .astype(jnp.bfloat16)
            .reshape(micro_seqs, block_len, kv_width)
        )
        key_all, value_all, segment_all = (
            lax.all_gather(key_rot, "ctx", axis=1, tiled=True),
            lax.all_gather(value_low, "ctx", axis=1, tiled=True),
            lax.all_gather(segment_part, "ctx", axis=1, tiled=True),
        )
        key_heads = key_all.reshape(micro_seqs, length, KV_HEADS, HEAD_DIM)
        value_heads = value_all.reshape(micro_seqs, length, KV_HEADS, HEAD_DIM)
        query_groups = query_rot.reshape(micro_seqs, block_len, KV_HEADS, groups, HEAD_DIM)
        allowed = (
            (segment_part[:, :, None] == segment_all[:, None, :])
            & (key_index[None, None, :] <= query_index[None, :, None])
        )[:, None, None]
        masked = masked_scores(query_groups, key_heads, allowed, score_scale)
        row_max = jnp.max(masked, axis=-1, keepdims=True)
        exponent = jnp.exp(masked - row_max)
        total = jnp.sum(exponent, axis=-1, keepdims=True)
        probs_low = (exponent / total).astype(jnp.bfloat16)
        log_total = row_max + jnp.log(total)
        attended = (
            jnp.einsum(
                "skgcl,slkd->sckgd", probs_low, value_heads, preferred_element_type=jnp.float32
            )
            .astype(jnp.bfloat16)
            .reshape(rows, attn_width)
        )
        resid = inputs + product(attended, out_weight)
        scale_ffn = rms_scale(resid)
        normed_ffn = (resid * scale_ffn * norm_ffn).astype(jnp.bfloat16)
        gate = product(normed_ffn, gate_weight)
        up = product(normed_ffn, up_weight)
        hidden = (jax.nn.silu(gate) * up).astype(jnp.bfloat16)
        outputs.append(
            (resid + product(hidden, down_weight))
            .astype(jnp.bfloat16)
            .reshape(micro_seqs, block_len, D)
        )
        query_weight, key_weight, value_weight, out_weight, gate_weight, up_weight, down_weight = (
            backward_weights()
        )
        down_grad = grad_out.astype(jnp.bfloat16)
        fresh_down = product_left(hidden, down_grad)
        hidden_grad = product_right(down_grad, down_weight)
        gate_sigmoid = jax.nn.sigmoid(gate)
        gate_grad = (hidden_grad * up * gate_sigmoid * (1.0 + gate * (1.0 - gate_sigmoid))).astype(
            jnp.bfloat16
        )
        up_grad = (hidden_grad * gate * gate_sigmoid).astype(jnp.bfloat16)
        fresh_gate = product_left(normed_ffn, gate_grad)
        fresh_up = product_left(normed_ffn, up_grad)
        normed_grad = product_right(gate_grad, gate_weight) + product_right(up_grad, up_weight)
        resid_grad, ffn_gain_grad = norm_back(resid, scale_ffn, norm_ffn, normed_grad)
        resid_grad = resid_grad + grad_out
        branch_grad = resid_grad.astype(jnp.bfloat16)
        fresh_out = product_left(attended, branch_grad)
        attended_grad = (
            product_right(branch_grad, out_weight)
            .astype(jnp.bfloat16)
            .reshape(micro_seqs, block_len, KV_HEADS, groups, HEAD_DIM)
        )
        probs = jnp.exp(masked_scores(query_groups, key_heads, allowed, score_scale) - log_total)
        probs_grad = jnp.einsum(
            "sckgd,slkd->skgcl", attended_grad, value_heads, preferred_element_type=jnp.float32
        )
        inner = jnp.sum(probs * probs_grad, axis=-1, keepdims=True)
        scores_grad = (probs * (probs_grad - inner)).astype(jnp.bfloat16)
        query_grad = (
            jnp.einsum(
                "skgcl,slkd->sckgd", scores_grad, key_heads, preferred_element_type=jnp.float32
            )
            * score_scale
        )
        key_part = (
            jnp.einsum(
                "skgcl,sckgd->slkd", scores_grad, query_groups, preferred_element_type=jnp.float32
            )
            * score_scale
        )
        value_part = jnp.einsum(
            "skgcl,sckgd->slkd",
            probs.astype(jnp.bfloat16),
            attended_grad,
            preferred_element_type=jnp.float32,
        )
        key_grad, value_grad = (
            lax.psum_scatter(
                key_part.reshape(micro_seqs, length, kv_width).astype(jnp.bfloat16),
                "ctx",
                scatter_dimension=1,
                tiled=True,
            ).astype(jnp.float32),
            lax.psum_scatter(
                value_part.reshape(micro_seqs, length, kv_width).astype(jnp.bfloat16),
                "ctx",
                scatter_dimension=1,
                tiled=True,
            ).astype(jnp.float32),
        )
        query_low = (
            rotate_back(query_grad.reshape(micro_seqs, block_len, HEADS, HEAD_DIM), cosine, sine)
            .astype(jnp.bfloat16)
            .reshape(rows, attn_width)
        )
        key_low = (
            rotate_back(key_grad.reshape(micro_seqs, block_len, KV_HEADS, HEAD_DIM), cosine, sine)
            .astype(jnp.bfloat16)
            .reshape(rows, kv_width)
        )
        value_grad_low = value_grad.astype(jnp.bfloat16).reshape(rows, kv_width)
        fresh_query = product_left(normed_attn, query_low)
        fresh_key = product_left(normed_attn, key_low)
        fresh_value = product_left(normed_attn, value_grad_low)
        attn_normed_grad = (
            product_right(query_low, query_weight)
            + product_right(key_low, key_weight)
            + product_right(value_grad_low, value_weight)
        )
        input_grad, attn_gain_grad = norm_back(inputs, scale_attn, norm_attn, attn_normed_grad)
        input_grads.append((input_grad + resid_grad).reshape(micro_seqs, block_len, D))
        attn_gain_total = attn_gain_total + attn_gain_grad
        ffn_gain_total = ffn_gain_total + ffn_gain_grad
        fresh = [fresh_query, fresh_key, fresh_value, fresh_out, fresh_gate, fresh_up, fresh_down]
        grad_totals = [running + piece for running, piece in zip(grad_totals, fresh)]
    shard_totals = reduce_at_end(grad_totals)
    attn_gain_sum, ffn_gain_sum = lax.psum((attn_gain_total, ffn_gain_total), ("dp", "ctx"))
    output = jnp.concatenate(outputs, axis=0)
    d_tokens = jnp.concatenate(input_grads, axis=0)
    return (
        output,
        d_tokens,
        attn_gain_sum,
        shard_totals[0],
        shard_totals[1],
        shard_totals[2],
        shard_totals[3],
        ffn_gain_sum,
        shard_totals[4],
        shard_totals[5],
        shard_totals[6],
    )


def solution(mesh):
    in_specs = (
        P("dp", "ctx", None),
        P("dp", "ctx"),
        P("dp", "ctx"),
        P(),
        P(("dp", "ctx")),
        P(("dp", "ctx")),
        P(("dp", "ctx")),
        P(("dp", "ctx")),
        P(),
        P(("dp", "ctx")),
        P(("dp", "ctx")),
        P(("dp", "ctx")),
        P("dp", "ctx", None),
    )
    out_specs = (
        P("dp", "ctx", None),
        P("dp", "ctx", None),
        P(),
        P(("dp", "ctx")),
        P(("dp", "ctx")),
        P(("dp", "ctx")),
        P(("dp", "ctx")),
        P(),
        P(("dp", "ctx")),
        P(("dp", "ctx")),
        P(("dp", "ctx")),
    )
    return jax.shard_map(body, mesh=mesh, in_specs=in_specs, out_specs=out_specs, check_vma=False)
```

profile of v0, /device:TPU:0, one launch (start us, length us, event | category | flops | bytes accessed | tf_op | source)
XLA Modules:
  0.0 967.7 jit_solution(10681395734420961702)
XLA Ops:
  13.2 47.4 %all-gather.4 = bf16[32,1,9600]{2,1,0:T(2,128)(2,1)S(1)} all-gather(bf16[1,1,9600]{2,1,0:T(2,128)(2,1)S(1)} %reshape.1609), channel_id=1, replica_groups=mesh['dp'=8,'ctx'=4] {'dp','ctx'}, dimensions={0}, use_global_device_ids=true | all-gather | bytes 633600 | tf_op jit(solution)/shard_map/all_gather | solution.py:168
  66.2 42.0 %all-gather.5 = bf16[32,1,9600]{2,1,0:T(2,128)(2,1)S(1)} all-gather(bf16[1,1,9600]{2,1,0:T(2,128)(2,1)S(1)} %reshape.1611), channel_id=1, replica_groups=mesh['dp'=8,'ctx'=4] {'dp','ctx'}, dimensions={0}, use_global_device_ids=true | all-gather | bytes 633600 | tf_op jit(solution)/shard_map/all_gather | solution.py:167
  117.0 8.5 all-gather.2
  126.8 10.4 %all-gather.3 = bf16[1024,320]{0,1:T(8,128)(2,1)S(1)} all-gather(bf16[256,320]{0,1:T(8,128)(2,1)S(1)} %fusion.106), channel_id=5, replica_groups=mesh['dp'=8,'ctx'=4] {'ctx'}, dimensions={0}, use_global_device_ids=true | all-gather | bytes 819200 | tf_op jit(solution)/shard_map/all_gather | solution.py:230
  137.3 5.1 all_gather.32
  142.3 5.1 all_gather.76
  147.4 8.4 all-gather
  155.9 8.7 all-gather.1
  166.0 39.5 %reduce.15 = bf16[32,28800]{1,0:T(8,128)(2,1)S(1)} reduce(bf16[32,1,28800]{2,1,0:T(2,128)(2,1)} %all-gather.20.cloned.1.call-done, bf16[]{:T(256)} %constant.80), dimensions={1}, to_apply=%all-gather.6.reduce_sub_computation | reduce | bytes 3686402 | tf_op jit(solution)/shard_map/all_gather | solution.py:166
  211.4 6.8 fusion.151
  218.2 7.7 fusion.6
  225.9 39.9 %reduce.16 = bf16[32,28800]{1,0:T(8,128)(2,1)S(1)} reduce(bf16[32,1,28800]{2,1,0:T(2,128)(2,1)} %all-gather.22.cloned.1.call-done, bf16[]{:T(256)} %constant.80), dimensions={1}, to_apply=%all-gather.7.reduce_sub_computation | reduce | bytes 3686402 | tf_op jit(solution)/shard_map/all_gather | solution.py:169
  268.6 8.7 fusion.44
  280.5 7.0 fusion.150
  287.5 7.6 fusion.7
  295.2 7.0 fusion.47
  304.5 10.0 %reshape.1537 = bf16[960,2560]{1,0:T(8,128)(2,1)} reshape(bf16[2457600]{0:T(1024)(128)(2,1)} %all-gather.14.cloned.1.call-done) | data formatting | bytes 9830400 | tf_op jit(solution)/shard_map/reshape | solution.py:174
  314.5 10.0 %reshape.1538 = bf16[960,2560]{1,0:T(8,128)(2,1)} reshape(bf16[2457600]{0:T(1024)(128)(2,1)} %all-gather.16.cloned.1.call-done) | data formatting | bytes 9830400 | tf_op jit(solution)/shard_map/reshape | solution.py:174
  324.4 5.6 fusion.152
  333.1 10.4 %all-gather.18.cloned.1.call-done = bf16[2457600]{0:T(1024)(128)(2,1)} async-done(((bf16[76800]{0:T(1024)(128)(2,1)}), bf16[2457600]{0:T(1024)(128)(2,1)}) %all-gather.18.cloned.1.call-update) | async-done | bytes 4915216 | tf_op jit(solution)/shard_map/all_gather | solution.py:172
  343.5 9.6 reshape.1539
  353.0 9.0 multiply_convert_fusion.2
  386.4 8.4 fusion
  394.7 7.9 fusion.17
  411.1 13.0 %fusion.3 = (f32[5,3,256]{2,1,0:T(4,128)S(1)}, f32[5,1024,256,3]{2,1,3,0:T(8,128)}) fusion(f32[1,5,3,256,1024]{3,4,2,1,0:T(8,128)} %get-tuple-element.82, f32[5,3,256]{2,1,0:T(4,128)S(1)} %log_add_fusion.1, bf16[1024,5,64,1]{0,2,3,1:T(8,128)(2,1)} %bitcast.417, bf16[256,5,3,64]{0,3,2,1:T(8,128)(2,1)S(1)} %bitcast.406), kind=kOutput, calls=%fused_computation.9 | convolution fusion | flops 515109120 | bytes 32634880 | tf_op jit(solution)/shard_map/sckgd,slkd->skgcl/dot_general | solution.py:289
  427.1 7.7 fusion.16
  448.0 9.1 fusion.37
  465.3 5.2 convert_element_type.480
  478.4 9.1 fusion.34
  489.6 5.3 convert_element_type.486
  497.8 6.6 fusion.158
  514.3 23.1 %all-to-all-done.3 = bf16[8,4,28800]{2,0,1:T(8,128)(2,1)} async-done(((bf16[8,4,28800]{2,0,1:T(8,128)(2,1)}), bf16[8,4,28800]{2,0,1:T(8,128)(2,1)}, u32[]{:S(2)}, u32[]{:S(2)}) %all-to-all-start.3) | async-done | bytes 1843232 | tf_op jit(solution)/shard_map/all_to_all | solution.py:89
  555.1 7.9 add_convert_fusion.2
  563.0 8.1 convert_element_type.488
  571.1 6.1 copy.57
  588.7 8.1 convert_element_type.490
  596.8 6.0 copy.58
  602.7 35.4 %all-to-all-done.4 = bf16[8,4,76800]{2,0,1:T(8,128)(2,1)} async-done(((bf16[8,4,76800]{2,0,1:T(8,128)(2,1)}), bf16[8,4,76800]{2,0,1:T(8,128)(2,1)}, u32[]{:S(2)}, u32[]{:S(2)}) %all-to-all-start.4) | async-done | bytes 4915232 | tf_op jit(solution)/shard_map/all_to_all | solution.py:92
  638.1 5.0 all-to-all-start.5
  649.7 7.9 copy.59
  657.6 10.0 %convert_element_type.492 = bf16[8,4,76800]{2,1,0:T(4,128)(2,1)} reshape(bf16[2560,960]{1,0:T(8,128)(2,1)} %copy.59) | data formatting | bytes 9830400 | tf_op jit(solution)/shard_map/convert_element_type | solution.py:99
  667.5 6.1 copy.60
  673.6 25.5 %all-to-all-done.5 = bf16[8,4,76800]{2,0,1:T(8,128)(2,1)} async-done(((bf16[8,4,76800]{2,0,1:T(8,128)(2,1)}), bf16[8,4,76800]{2,0,1:T(8,128)(2,1)}, u32[]{:S(2)}, u32[]{:S(2)}) %all-to-all-start.5) | async-done | bytes 4915232 | tf_op jit(solution)/shard_map/all_to_all | solution.py:95
  699.1 5.0 all-to-all-start.6
  721.3 38.7 %all-to-all-done.6 = bf16[8,4,76800]{2,0,1:T(8,128)(2,1)} async-done(((bf16[8,4,76800]{2,0,1:T(8,128)(2,1)}), bf16[8,4,76800]{2,0,1:T(8,128)(2,1)}, u32[]{:S(2)}, u32[]{:S(2)}) %all-to-all-start.6) | async-done | bytes 4915232 | tf_op jit(solution)/shard_map/all_to_all | solution.py:98
  765.9 5.2 fusion.58
  783.1 45.0 %all-reduce.7 = (f32[960]{0:T(1024)}, f32[960]{0:T(1024)}) all-reduce(f32[960]{0:T(1024)S(1)} %add.336, f32[960]{0:T(1024)S(1)} %add.341), channel_id=1, replica_groups=mesh['dp'=8,'ctx'=4] {'dp','ctx'}, use_global_device_ids=true, to_apply=%region_20.21 | all-reduce | flops 1920 | bytes 15360 | tf_op jit(solution)/shard_map/psum | solution.py:352
  831.8 109.9 %all-reduce.11.cloned.1.call-done = (bf16[8,28800]{1,0:T(8,128)(2,1)}, bf16[8,9600]{1,0:T(8,128)(2,1)}, bf16[8,9600]{1,0:T(8,128)(2,1)}, bf16[8,28800]{1,0:T(8,1...) async-done(((bf16[8,28800]{1,0:T(8,128)(2,1)}, bf16[8,9600]{1,0:T(8,128)(2,1)}, bf16[8,9600]{1,0:T(8,128)(2,1)}, ...) | async-done | bytes 4915216
  (375 shorter events, 212.1 us)
Async XLA Ops:
  7.2 58.8 %copy-start.1 = (bf16[2,256,960]{1,2,0:T(8,128)(2,1)S(1)}, bf16[2,256,960]{1,2,0:T(8,128)(2,1)}, u32[]{:S(2)}) copy-start(bf16[2,256,960]{1,2,0:T(8,128)(2,1)} %param.13) | copy-start | bytes 2949124
  7.2 59.0 %copy-start.85 = (bf16[9600]{0:T(1024)(128)(2,1)S(1)}, bf16[9600]{0:T(1024)(128)(2,1)}, u32[]{:S(2)}) copy-start(bf16[9600]{0:T(1024)(128)(2,1)} %param.18) | copy-start | bytes 57604
  7.2 158.8 %all-gather.20.cloned.1.call-start = ((), (), s32[]{:S(2)}) async-start(), calls=%async_computation.18 | async-start | bytes 3801600 | tf_op jit(solution)/shard_map/all_gather | solution.py:166
  8.9 217.0 %all-gather.22.cloned.1.call-start = ((), (), s32[]{:S(2)}) async-start(), calls=%async_computation.19 | async-start | bytes 3801600 | tf_op jit(solution)/shard_map/all_gather | solution.py:169
  10.5 294.0 %all-gather.14.cloned.1.call-start = ((), (), s32[]{:S(2)}) async-start(), calls=%async_computation.11 | async-start | bytes 5068800 | tf_op jit(solution)/shard_map/all_gather | solution.py:170
  11.2 303.2 %all-gather.16.cloned.1.call-start = ((), (), s32[]{:S(2)}) async-start(), calls=%async_computation.12 | async-start | bytes 5068800 | tf_op jit(solution)/shard_map/all_gather | solution.py:171
  11.8 331.7 %all-gather.18.cloned.1.call-start = ((), (), s32[]{:S(2)}) async-start(), calls=%async_computation.13 | async-start | bytes 5068800 | tf_op jit(solution)/shard_map/all_gather | solution.py:172
  12.4 492.0 %reduce-scatter.9.cloned.1.call-start = ((), (), s32[]{:S(2)}) async-start(), calls=%async_computation.16 | async-start | bytes 819200 | tf_op jit(solution)/shard_map/reduce_scatter | solution.py:313
  60.6 52.8 %copy-start.72 = (f32[960]{0:T(1024)S(1)}, f32[960]{0:T(1024)}, u32[]{:S(2)}) copy-start(f32[960]{0:T(1024)} %param.16) | copy-start | bytes 11524
  113.4 94.9 %copy-start.80 = (f32[256]{0:T(256)}, f32[256]{0:T(256)S(1)}, u32[]{:S(2)}) copy-start(f32[256]{0:T(256)S(1)} %get-tuple-element.94) | copy-start | bytes 3076
  115.1 10.4 %copy-start.90 = (s32[2,256]{1,0:T(2,128)S(1)}, s32[2,256]{1,0:T(2,128)}, u32[]{:S(2)}) copy-start(s32[2,256]{1,0:T(2,128)} %param.15) | copy-start | bytes 6148
  115.8 21.5 %copy-start.91 = (s32[2,256]{1,0:T(2,128)S(1)}, s32[2,256]{1,0:T(2,128)}, u32[]{:S(2)}) copy-start(s32[2,256]{1,0:T(2,128)} %param.14) | copy-start | bytes 6148
  126.2 39.8 %copy-start.49 = (f32[256,64]{0,1:T(8,128)}, f32[256,64]{0,1:T(8,128)S(1)}, u32[]{:S(2)}) copy-start(f32[256,64]{0,1:T(8,128)S(1)} %get-tuple-element.58) | copy-start | bytes 196612
  126.2 85.0 %copy-start.45 = (f32[256,64]{0,1:T(8,128)}, f32[256,64]{0,1:T(8,128)S(1)}, u32[]{:S(2)}) copy-start(f32[256,64]{0,1:T(8,128)S(1)} %get-tuple-element.59) | copy-start | bytes 196612
  137.3 143.2 %copy-start.14 = (bf16[1024,320]{0,1:T(8,128)(2,1)}, bf16[1024,320]{0,1:T(8,128)(2,1)S(1)}, u32[]{:S(2)}) copy-start(bf16[1024,320]{0,1:T(8,128)(2,1)S(1)} %all-gather.3) | copy-start | bytes 1966084
  218.2 50.4 %copy-start.74 = (f32[5,3,256]{2,1,0:T(4,128)}, f32[5,3,256]{2,1,0:T(4,128)S(1)}, u32[]{:S(2)}) copy-start(f32[5,3,256]{2,1,0:T(4,128)S(1)} %get-tuple-element.81) | copy-start | bytes 46084
  225.9 42.7 %copy-start.77 = (f32[5,3,256]{2,1,0:T(4,128)}, f32[5,3,256]{2,1,0:T(4,128)S(1)}, u32[]{:S(2)}) copy-start(f32[5,3,256]{2,1,0:T(4,128)S(1)} %fusion.6) | copy-start | bytes 46084
  268.6 8.7 copy-start.2
  278.3 26.0 %copy-start.11 = (f32[256,960]{0,1:T(8,128)}, f32[256,960]{0,1:T(8,128)S(1)}, u32[]{:S(2)}) copy-start(f32[256,960]{0,1:T(8,128)S(1)} %get-tuple-element.84) | copy-start | bytes 2949124
  333.1 19.9 %copy-start.26 = (bf16[2,256,960]{1,2,0:T(8,128)(2,1)S(1)}, bf16[2,256,960]{1,2,0:T(8,128)(2,1)}, u32[]{:S(2)}) copy-start(bf16[2,256,960]{1,2,0:T(8,128)(2,1)} %param.25) | copy-start | bytes 2949124
  343.5 23.5 %slice-start.8 = ((s8[4915200]{0:T(1024)(128)(4,1)}), s8[720896]{0:T(1024)(128)(4,1)S(1)}, s32[]{:S(2)}) async-start(s8[4915200]{0:T(1024)(128)(4,1)} %bitcast.400), calls=%async_computation.29 | async-start | bytes 1441792
  353.0 14.0 %slice-start.9 = ((s8[4915200]{0:T(1024)(128)(4,1)}), s8[4194304]{0:T(1024)(128)(4,1)S(1)}, s32[]{:S(2)}) async-start(s8[4915200]{0:T(1024)(128)(4,1)} %bitcast.400), calls=%async_computation.30 | async-start | bytes 8388608
  362.1 8.1 slice-start.10
  377.6 8.0 slice-start.4
  394.7 7.9 copy-start.15
  408.5 96.9 %reduce-scatter.5.cloned.1.call-start = ((), (), s32[]{:S(2)}) async-start(), calls=%async_computation.14 | async-start | bytes 819200 | tf_op jit(solution)/shard_map/reduce_scatter | solution.py:313
  411.1 13.1 %slice-start = ((s8[15728640]{0:T(1024)(128)(4,1)}), s8[4194304]{0:T(1024)(128)(4,1)S(1)}, s32[]{:S(2)}) async-start(s8[15728640]{0:T(1024)(128)(4,1)} %bitcast.396), calls=%async_computation.21 | async-start | bytes 8388608
  411.1 13.7 %slice-start.1 = ((s8[15728640]{0:T(1024)(128)(4,1)}), s8[4194304]{0:T(1024)(128)(4,1)S(1)}, s32[]{:S(2)}) async-start(s8[15728640]{0:T(1024)(128)(4,1)} %bitcast.396), calls=%async_computation.22 | async-start | bytes 8388608
  411.1 15.2 %slice-start.2 = ((s8[15728640]{0:T(1024)(128)(4,1)}), s8[4194304]{0:T(1024)(128)(4,1)S(1)}, s32[]{:S(2)}) async-start(s8[15728640]{0:T(1024)(128)(4,1)} %bitcast.396), calls=%async_computation.23 | async-start | bytes 8388608
  411.1 16.0 %slice-start.3 = ((s8[15728640]{0:T(1024)(128)(4,1)}), s8[3145728]{0:T(1024)(128)(4,1)S(1)}, s32[]{:S(2)}) async-start(s8[15728640]{0:T(1024)(128)(4,1)} %bitcast.396), calls=%async_computation.24 | async-start | bytes 6291456
  442.9 98.7 %reduce-scatter.7.cloned.1.call-start = ((), (), s32[]{:S(2)}) async-start(), calls=%async_computation.15 | async-start | bytes 819200 | tf_op jit(solution)/shard_map/reduce_scatter | solution.py:319
  448.0 9.1 copy-start.84
  473.5 32.9 %all-to-all-start = ((bf16[8,4,28800]{2,0,1:T(8,128)(2,1)}), bf16[8,4,28800]{2,0,1:T(8,128)(2,1)}, u32[]{:S(2)}, u32[]{:S(2)}) async-start(bf16[8,4,28800]{2,0,1:T(8,128)(2,1)} %copy.51), calls=%async_computation.4 | async-start | bytes 3686400 | tf_op jit(solution)/shard_map/all_to_all | solution.py:80
  477.9 9.6 copy-start.69
  477.9 66.1 %reduce-scatter.11.cloned.1.call-start = ((), (), s32[]{:S(2)}) async-start(), calls=%async_computation.17 | async-start | bytes 819200 | tf_op jit(solution)/shard_map/reduce_scatter | solution.py:319
  478.4 9.2 copy-start.5
  478.4 9.2 copy-start.7
  506.5 31.0 %all-to-all-start.3 = ((bf16[8,4,28800]{2,0,1:T(8,128)(2,1)}), bf16[8,4,28800]{2,0,1:T(8,128)(2,1)}, u32[]{:S(2)}, u32[]{:S(2)}) async-start(bf16[8,4,28800]{2,0,1:T(8,128)(2,1)} %copy.56), calls=%async_computation.7 | async-start | bytes 3686400 | tf_op jit(solution)/shard_map/all_to_all | solution.py:89
  537.4 14.0 %all-to-all-start.1 = ((bf16[8,4,9600]{2,0,1:T(8,128)(2,1)}), bf16[8,4,9600]{2,0,1:T(8,128)(2,1)}, u32[]{:S(2)}, u32[]{:S(2)}) async-start(bf16[8,4,9600]{2,0,1:T(8,128)(2,1)} %copy.53), calls=%async_computation.5 | async-start | bytes 1228800 | tf_op jit(solution)/shard_map/all_to_all | solution.py:83
  551.5 25.7 %all-to-all-start.2 = ((bf16[8,4,9600]{2,0,1:T(8,128)(2,1)}), bf16[8,4,9600]{2,0,1:T(8,128)(2,1)S(1)}, u32[]{:S(2)}, u32[]{:S(2)}) async-start(bf16[8,4,9600]{2,0,1:T(8,128)(2,1)} %copy.55), calls=%async_computation.6 | async-start | bytes 1228800 | tf_op jit(solution)/shard_map/all_to_all | solution.py:86
  577.2 60.9 %all-to-all-start.4 = ((bf16[8,4,76800]{2,0,1:T(8,128)(2,1)}), bf16[8,4,76800]{2,0,1:T(8,128)(2,1)}, u32[]{:S(2)}, u32[]{:S(2)}) async-start(bf16[8,4,76800]{2,0,1:T(8,128)(2,1)} %copy.57), calls=%async_computation.8 | async-start | bytes 9830400 | tf_op jit(solution)/shard_map/all_to_all | solution.py:92
  602.7 40.4 %copy-start.29 = (bf16[2,256,960]{1,2,0:T(8,128)(2,1)S(1)}, bf16[2,256,960]{1,2,0:T(8,128)(2,1)}, u32[]{:S(2)}) copy-start(bf16[2,256,960]{1,2,0:T(8,128)(2,1)} %param.25) | copy-start | bytes 2949124
  638.1 61.0 %all-to-all-start.5 = ((bf16[8,4,76800]{2,0,1:T(8,128)(2,1)}), bf16[8,4,76800]{2,0,1:T(8,128)(2,1)}, u32[]{:S(2)}, u32[]{:S(2)}) async-start(bf16[8,4,76800]{2,0,1:T(8,128)(2,1)} %copy.58), calls=%async_computation.9 | async-start | bytes 9830400 | tf_op jit(solution)/shard_map/all_to_all | solution.py:95
  699.1 61.0 %all-to-all-start.6 = ((bf16[8,4,76800]{2,0,1:T(8,128)(2,1)}), bf16[8,4,76800]{2,0,1:T(8,128)(2,1)}, u32[]{:S(2)}, u32[]{:S(2)}) async-start(bf16[8,4,76800]{2,0,1:T(8,128)(2,1)} %copy.60), calls=%async_computation.10 | async-start | bytes 9830400 | tf_op jit(solution)/shard_map/all_to_all | solution.py:98
  704.1 237.6 %all-reduce.11.cloned.1.call-start = ((), (), s32[]{:S(2)}) async-start(), calls=%async_computation.20 | async-start | bytes 9830400
  780.0 48.1 %copy-start.6 = (f32[256,960]{0,1:T(8,128)S(1)}, f32[256,960]{0,1:T(8,128)}, u32[]{:S(2)}) copy-start(f32[256,960]{0,1:T(8,128)} %copy-done.4) | copy-start | bytes 2949124
  780.0 48.1 %copy-start.87 = (f32[256]{0:T(256)S(1)}, f32[256]{0:T(256)}, u32[]{:S(2)}) copy-start(f32[256]{0:T(256)} %get-tuple-element.69) | copy-start | bytes 3076
  780.0 48.1 %copy-start.88 = (f32[256]{0:T(256)S(1)}, f32[256]{0:T(256)}, u32[]{:S(2)}) copy-start(f32[256]{0:T(256)} %get-tuple-element.95) | copy-start | bytes 3076
  (76 other events, 232.2 us)
Sparse Core Ops, SparseCore 0:
  11.5 66.7 all-gather.19
  81.8 60.0 all-gather.21
  144.7 66.9 all-gather.13
  214.3 63.1 all-gather.15
  280.2 63.2 all-gather.17
  408.7 21.2 reduce-scatter.8
  443.0 21.2 reduce-scatter.4
  466.9 26.0 reduce-scatter.6
  497.9 26.2 reduce-scatter.10
  764.7 176.9 all-reduce.10
where the time goes:
time: 976 us; the launch traced here: 968 us
  waiting for transfers between devices  249 us (26%)
  matrix products  188 us (19%)
  blocking collectives  180 us (18%)
  other arithmetic  175 us (18%)
  local copies, waits for them, and re-layouts  126 us (13%)
  starting transfers between devices  32.6 us (3%)
  between operations  16 us (2%)
    unnamed x11, waiting for transfers between devices  112 us
    all_gather x1, blocking collectives, forward_weights(): lax.all_gather(w_value, ('dp', 'ctx'), axis=0, tiled=True)  47.4 us
    dot_general x14, matrix products, product_left(): lax.dot_general(left, right, (((0,), (0,)), ((), ())), preferred_element_...  45.5 us
    psum x1, blocking collectives, body(): lax.psum((attn_gain_total, ffn_gain_total), ('dp', 'ctx'))  45 us
    all_gather x1, blocking collectives, forward_weights(): lax.all_gather(w_key, ('dp', 'ctx'), axis=0, tiled=True)  42 us
    all_gather x1, other arithmetic, forward_weights(): lax.all_gather(w_out, ('dp', 'ctx'), axis=0, tiled=True)  39.9 us
    all_gather x1, other arithmetic, forward_weights(): lax.all_gather(w_query, ('dp', 'ctx'), axis=0, tiled=True)  39.5 us
    all_to_all x1, waiting for transfers between devices, reduce_at_end(): lax.all_to_all(blocks[6].astype(jnp.bfloat16), 'ctx', split_axis=1, conca...  38.7 us
  transfers between devices with their start and end apart: 17, of which 7 were waited for; matrix products, arithmetic and copies ran while one was open for 40% of the time, Pallas kernels for 0%

commit v1 on v0

--- a/solution.py
+++ b/solution.py
@@ -14,6 +14,28 @@
 mask_fill = -1000000000.0
 
 
+def in_blocks(value, dim, size):
+    before, after = (value.shape[:dim], value.shape[dim + 1 :])
+    return jnp.moveaxis(value.reshape(*before, size, -1, *after), dim, 0)
+
+
+def joined_along(blocks, dim):
+    shape = list(blocks.shape[1:])
+    shape[dim] *= blocks.shape[0]
+    return jnp.moveaxis(blocks, 0, dim).reshape(shape)
+
+
+def pairwise_exchange(x, axis, split_dim, concat_dim):
+    size, position = (lax.axis_size(axis), lax.axis_index(axis))
+    pieces = in_blocks(x, split_dim, size)
+    gathered = [pieces[position]]
+    for step in range(1, size):
+        sent = pieces[position ^ step]
+        gathered.append(lax.ppermute(sent, axis, [(i, i ^ step) for i in range(size)]))
+    pieces = jnp.stack(gathered)[position ^ jnp.arange(size)]
+    return joined_along(pieces, concat_dim)
+
+
 def rms_scale(values):
     return lax.rsqrt(jnp.mean(values * values, axis=-1, keepdims=True) + norm_eps)
 
@@ -92,9 +114,7 @@
         lax.all_to_all(
             blocks[4].astype(jnp.bfloat16), "ctx", split_axis=1, concat_axis=1, tiled=True
         ).astype(jnp.float32),
-        lax.all_to_all(
-            blocks[5].astype(jnp.bfloat16), "ctx", split_axis=1, concat_axis=1, tiled=True
-        ).astype(jnp.float32),
+        pairwise_exchange(blocks[5].astype(jnp.bfloat16), "ctx", 1, 1).astype(jnp.float32),
         lax.all_to_all(
             blocks[6].astype(jnp.bfloat16), "ctx", split_axis=1, concat_axis=1, tiled=True
         ).astype(jnp.float32),

time: 976 us -> 980 us (level)
  local copies, waits for them, and re-layouts: 126 us -> 145 us
  waiting for transfers between devices: 249 us -> 230 us
    ppermute x0 -> x3, waiting for transfers between devices: none -> 47.6 us  [pairwise_exchange(): lax.ppermute(sent, axis, [(i, i ^ step) for i in range(size)])]
    all_to_all x1, waiting for transfers between devices: 35.4 us -> 7.12 us  [reduce_at_end(): lax.all_to_all(blocks[4].astype(jnp.bfloat16), 'ctx', split_axis=1, conca...]
    all_to_all x1 -> x0, waiting for transfers between devices: 25.5 us -> none  [reduce_at_end(): lax.all_to_all(blocks[5].astype(jnp.bfloat16), 'ctx', split_axis=1, conca...]
    all_to_all x1, waiting for transfers between devices: 38.7 us -> 24.5 us  [reduce_at_end(): lax.all_to_all(blocks[6].astype(jnp.bfloat16), 'ctx', split_axis=1, conca...]
    another operation x0 -> x1, local copies, waits for them, and re-layouts: none -> 13.4 us
    another operation x2 -> x3, other arithmetic: 15.6 us -> 21 us
  transfers between devices with their start and end apart: 17 -> 19, of which waited for: 7 -> 8; matrix products, arithmetic and copies ran while one was open for 40% -> 43% of each run, Pallas kernels for 0% -> 0%
where the time goes in v1:
time: 980 us; the launch traced here: 971 us
  waiting for transfers between devices  230 us (23%)
  matrix products  194 us (20%)
  blocking collectives  179 us (18%)
  other arithmetic  178 us (18%)
  local copies, waits for them, and re-layouts  145 us (15%)
  starting transfers between devices  29.8 us (3%)
  between operations  16 us (2%)
    unnamed x11, waiting for transfers between devices  112 us
    dot_general x14, matrix products, product_left(): lax.dot_general(left, right, (((0,), (0,)), ((), ())), preferred_element_...  48.8 us
    ppermute x3, waiting for transfers between devices, pairwise_exchange(): lax.ppermute(sent, axis, [(i, i ^ step) for i in range(size)])  47.6 us
    all_gather x1, blocking collectives, forward_weights(): lax.all_gather(w_value, ('dp', 'ctx'), axis=0, tiled=True)  47.4 us
    psum x1, blocking collectives, body(): lax.psum((attn_gain_total, ffn_gain_total), ('dp', 'ctx'))  44.7 us
    all_gather x1, blocking collectives, forward_weights(): lax.all_gather(w_key, ('dp', 'ctx'), axis=0, tiled=True)  42.1 us
    all_gather x1, other arithmetic, forward_weights(): lax.all_gather(w_out, ('dp', 'ctx'), axis=0, tiled=True)  39.9 us
    all_gather x1, other arithmetic, forward_weights(): lax.all_gather(w_query, ('dp', 'ctx'), axis=0, tiled=True)  39.5 us
  transfers between devices with their start and end apart: 19, of which 8 were waited for; matrix products, arithmetic and copies ran while one was open for 43% of the time, Pallas kernels for 0%

profile of v1, /device:TPU:0, one launch (start us, length us, event | category | flops | bytes accessed | tf_op | source)
XLA Modules:
  0.0 971.4 jit_solution(5822365467697926759)
XLA Ops:
  13.2 47.4 %all-gather.4 = bf16[32,1,9600]{2,1,0:T(2,128)(2,1)S(1)} all-gather(bf16[1,1,9600]{2,1,0:T(2,128)(2,1)S(1)} %reshape.1655), channel_id=1, replica_groups=mesh['dp'=8,'ctx'=4] {'dp','ctx'}, dimensions={0}, use_global_device_ids=true | all-gather | bytes 633600 | tf_op jit(solution)/shard_map/all_gather | solution.py:188
  66.2 42.1 %all-gather.5 = bf16[32,1,9600]{2,1,0:T(2,128)(2,1)S(1)} all-gather(bf16[1,1,9600]{2,1,0:T(2,128)(2,1)S(1)} %reshape.1657), channel_id=1, replica_groups=mesh['dp'=8,'ctx'=4] {'dp','ctx'}, dimensions={0}, use_global_device_ids=true | all-gather | bytes 633600 | tf_op jit(solution)/shard_map/all_gather | solution.py:187
  118.4 8.5 all-gather.2
  128.1 9.6 all-gather.3
  147.9 8.4 all-gather
  156.5 8.2 all-gather.1
  166.1 39.5 %reduce.19 = bf16[32,28800]{1,0:T(8,128)(2,1)S(1)} reduce(bf16[32,1,28800]{2,1,0:T(2,128)(2,1)} %all-gather.20.cloned.1.call-done, bf16[]{:T(256)} %constant.92), dimensions={1}, to_apply=%all-gather.6.reduce_sub_computation | reduce | bytes 3686402 | tf_op jit(solution)/shard_map/all_gather | solution.py:186
  211.4 6.8 fusion.152
  218.3 7.7 fusion.6
  226.0 39.9 %reduce.20 = bf16[32,28800]{1,0:T(8,128)(2,1)S(1)} reduce(bf16[32,1,28800]{2,1,0:T(2,128)(2,1)} %all-gather.22.cloned.1.call-done, bf16[]{:T(256)} %constant.92), dimensions={1}, to_apply=%all-gather.7.reduce_sub_computation | reduce | bytes 3686402 | tf_op jit(solution)/shard_map/all_gather | solution.py:189
  268.7 7.2 fusion.44
  279.1 6.9 fusion.151
  286.1 7.8 fusion.7
  293.8 7.0 fusion.47
  303.1 10.0 %reshape.1572 = bf16[960,2560]{1,0:T(8,128)(2,1)} reshape(bf16[2457600]{0:T(1024)(128)(2,1)} %all-gather.14.cloned.1.call-done) | data formatting | bytes 9830400 | tf_op jit(solution)/shard_map/reshape | solution.py:194
  313.1 10.0 %reshape.1573 = bf16[960,2560]{1,0:T(8,128)(2,1)} reshape(bf16[2457600]{0:T(1024)(128)(2,1)} %all-gather.16.cloned.1.call-done) | data formatting | bytes 9830400 | tf_op jit(solution)/shard_map/reshape | solution.py:194
  323.1 5.6 fusion.153
  331.7 11.4 %all-gather.18.cloned.1.call-done = bf16[2457600]{0:T(1024)(128)(2,1)} async-done(((bf16[76800]{0:T(1024)(128)(2,1)}), bf16[2457600]{0:T(1024)(128)(2,1)}) %all-gather.18.cloned.1.call-update) | async-done | bytes 4915216 | tf_op jit(solution)/shard_map/all_gather | solution.py:192
  343.1 9.6 reshape.1574
  352.7 8.9 multiply_convert_fusion.2
  385.8 8.4 fusion
  394.1 8.1 fusion.17
  410.8 13.0 %fusion.3 = (f32[5,3,256]{2,1,0:T(4,128)S(1)}, f32[5,1024,256,3]{2,1,3,0:T(8,128)}) fusion(f32[1,5,3,256,1024]{3,4,2,1,0:T(8,128)} %get-tuple-element.86, f32[5,3,256]{2,1,0:T(4,128)S(1)} %log_add_fusion.1, bf16[1024,5,64,1]{0,2,3,1:T(8,128)(2,1)} %bitcast.436, bf16[256,5,3,64]{0,3,2,1:T(8,128)(2,1)S(1)} %bitcast.425), kind=kOutput, calls=%fused_computation.10 | convolution fusion | flops 515109120 | bytes 32634880 | tf_op jit(solution)/shard_map/sckgd,slkd->skgcl/dot_general | solution.py:309
  426.8 7.6 fusion.16
  442.5 5.3 convert_element_type.487
  459.3 6.7 fusion.32
  470.7 5.3 convert_element_type.493
  484.2 8.9 fusion.37
  493.5 9.0 fusion.34
  502.5 7.6 add_convert_fusion.2
  510.1 8.1 convert_element_type.495
  518.2 6.1 copy.61
  524.3 6.6 fusion.160
  540.6 23.4 %all-to-all-done.3 = bf16[8,4,28800]{2,0,1:T(8,128)(2,1)} async-done(((bf16[8,4,28800]{2,0,1:T(8,128)(2,1)}), bf16[8,4,28800]{2,0,1:T(8,128)(2,1)}, u32[]{:S(2)}, u32[]{:S(2)}) %all-to-all-start.3) | async-done | bytes 1843232 | tf_op jit(solution)/shard_map/all_to_all | solution.py:111
  581.9 7.8 add_convert_fusion.1
  589.8 8.1 convert_element_type.497
  602.9 13.4 %constant_dynamic-slice_fusion.3 = (bf16[8,1,1,76800]{3,1,0,2:T(2,128)(2,1)S(1)}, bf16[8,1,1,76800]{3,1,0,2:T(2,128)(2,1)S(1)}, bf16[8,1,1,76800]{3,1,0,2:T(2,128)(2,1)S(1)}, bf16[8,1,1,76800]{3,1,0,2:T(2,128)(2,1)S(1)}) fusion(bf16[8,4,1,76800]{3,1,0,2:T(4,128)(2,1)} %convert_element_type.497, s32[]{:T(128)S(6)} %select_n.33, s32[]{:T(128)S(6)} %select_n.35, ...), kind=kLoop, calls=%fused_computation.229 | loop fusion | bytes 9830416 | tf_op jit(solution)/shard_map/dynamic-slice
  628.4 7.9 copy.66
  636.2 9.9 %convert_element_type.499 = bf16[8,4,76800]{2,1,0:T(4,128)(2,1)} reshape(bf16[2560,960]{1,0:T(8,128)(2,1)} %copy.66) | data formatting | bytes 9830400 | tf_op jit(solution)/shard_map/convert_element_type | solution.py:119
  646.2 6.1 copy.67
  652.2 7.1 all-to-all-done.4
  664.4 20.3 %collective-permute-done.2 = bf16[8,1,76800]{2,0,1:T(8,128)(2,1)} collective-permute-done((bf16[8,1,76800]{2,0,1:T(8,128)(2,1)}, bf16[8,1,76800]{2,0,1:T(8,128)(2,1)}, u32[]{:S(2)}, u32[]{:S(2)}) %collective-permute-start.2) | collective-permute-done | bytes 1228832 | tf_op jit(solution)/shard_map/ppermute | solution.py:34
  684.7 27.3 %collective-permute-done.1 = bf16[8,1,76800]{2,0,1:T(8,128)(2,1)} collective-permute-done((bf16[8,1,76800]{2,0,1:T(8,128)(2,1)}, bf16[8,1,76800]{2,0,1:T(8,128)(2,1)}, u32[]{:S(2)}, u32[]{:S(2)}) %collective-permute-start.1) | collective-permute-done | bytes 1228832 | tf_op jit(solution)/shard_map/ppermute | solution.py:34
  712.0 5.2 maximum_bitcast_fusion
  717.2 5.5 gather_fusion
  739.7 24.5 %all-to-all-done.5 = bf16[8,4,76800]{2,0,1:T(8,128)(2,1)} async-done(((bf16[8,4,76800]{2,0,1:T(8,128)(2,1)}), bf16[8,4,76800]{2,0,1:T(8,128)(2,1)}, u32[]{:S(2)}, u32[]{:S(2)}) %all-to-all-start.5) | async-done | bytes 4915232 | tf_op jit(solution)/shard_map/all_to_all | solution.py:118
  787.4 44.7 %all-reduce.7 = (f32[960]{0:T(1024)}, f32[960]{0:T(1024)}) all-reduce(f32[960]{0:T(1024)S(1)} %add.358, f32[960]{0:T(1024)S(1)} %add.363), channel_id=1, replica_groups=mesh['dp'=8,'ctx'=4] {'dp','ctx'}, use_global_device_ids=true, to_apply=%region_20.21 | all-reduce | flops 1920 | bytes 15360 | tf_op jit(solution)/shard_map/psum | solution.py:372
  835.8 110.0 %all-reduce.11.cloned.1.call-done = (bf16[8,28800]{1,0:T(8,128)(2,1)}, bf16[8,9600]{1,0:T(8,128)(2,1)}, bf16[8,9600]{1,0:T(8,128)(2,1)}, bf16[8,28800]{1,0:T(8,1...) async-done(((bf16[8,28800]{1,0:T(8,128)(2,1)}, bf16[8,9600]{1,0:T(8,128)(2,1)}, bf16[8,9600]{1,0:T(8,128)(2,1)}, ...) | async-done | bytes 4915216
  (383 shorter events, 230.8 us)
Async XLA Ops:
  7.2 58.8 %copy-start.2 = (bf16[2,256,960]{1,2,0:T(8,128)(2,1)S(1)}, bf16[2,256,960]{1,2,0:T(8,128)(2,1)}, u32[]{:S(2)}) copy-start(bf16[2,256,960]{1,2,0:T(8,128)(2,1)} %param.13) | copy-start | bytes 2949124
  7.2 59.0 %copy-start.82 = (bf16[9600]{0:T(1024)(128)(2,1)S(1)}, bf16[9600]{0:T(1024)(128)(2,1)}, u32[]{:S(2)}) copy-start(bf16[9600]{0:T(1024)(128)(2,1)} %param.18) | copy-start | bytes 57604
  7.2 158.9 %all-gather.20.cloned.1.call-start = ((), (), s32[]{:S(2)}) async-start(), calls=%async_computation.17 | async-start | bytes 3801600 | tf_op jit(solution)/shard_map/all_gather | solution.py:186
  8.9 217.1 %all-gather.22.cloned.1.call-start = ((), (), s32[]{:S(2)}) async-start(), calls=%async_computation.18 | async-start | bytes 3801600 | tf_op jit(solution)/shard_map/all_gather | solution.py:189
  10.5 292.6 %all-gather.14.cloned.1.call-start = ((), (), s32[]{:S(2)}) async-start(), calls=%async_computation.10 | async-start | bytes 5068800 | tf_op jit(solution)/shard_map/all_gather | solution.py:190
  11.2 301.9 %all-gather.16.cloned.1.call-start = ((), (), s32[]{:S(2)}) async-start(), calls=%async_computation.11 | async-start | bytes 5068800 | tf_op jit(solution)/shard_map/all_gather | solution.py:191
  11.8 331.3 %all-gather.18.cloned.1.call-start = ((), (), s32[]{:S(2)}) async-start(), calls=%async_computation.12 | async-start | bytes 5068800 | tf_op jit(solution)/shard_map/all_gather | solution.py:192
  12.4 518.5 %reduce-scatter.9.cloned.1.call-start = ((), (), s32[]{:S(2)}) async-start(), calls=%async_computation.15 | async-start | bytes 819200 | tf_op jit(solution)/shard_map/reduce_scatter | solution.py:333
  60.6 52.9 %copy-start.72 = (f32[960]{0:T(1024)S(1)}, f32[960]{0:T(1024)}, u32[]{:S(2)}) copy-start(f32[960]{0:T(1024)} %param.16) | copy-start | bytes 11524
  113.5 94.8 %copy-start.77 = (f32[256]{0:T(256)}, f32[256]{0:T(256)S(1)}, u32[]{:S(2)}) copy-start(f32[256]{0:T(256)S(1)} %get-tuple-element.98) | copy-start | bytes 3076
  115.2 11.6 %copy-start.87 = (s32[2,256]{1,0:T(2,128)S(1)}, s32[2,256]{1,0:T(2,128)}, u32[]{:S(2)}) copy-start(s32[2,256]{1,0:T(2,128)} %param.15) | copy-start | bytes 6148
  115.9 21.9 %copy-start.88 = (s32[2,256]{1,0:T(2,128)S(1)}, s32[2,256]{1,0:T(2,128)}, u32[]{:S(2)}) copy-start(s32[2,256]{1,0:T(2,128)} %param.14) | copy-start | bytes 6148
  117.1 30.8 %copy-start.75 = (bf16[256,320]{0,1:T(8,128)(2,1)S(1)}, bf16[256,320]{0,1:T(8,128)(2,1)}, u32[]{:S(2)}) copy-start(bf16[256,320]{0,1:T(8,128)(2,1)} %convolution_convert_fusion.3) | copy-start | bytes 491524
  127.5 28.9 %copy-start.49 = (f32[256,64]{0,1:T(8,128)}, f32[256,64]{0,1:T(8,128)S(1)}, u32[]{:S(2)}) copy-start(f32[256,64]{0,1:T(8,128)S(1)} %get-tuple-element.62) | copy-start | bytes 196612
  127.5 28.9 %copy-start.52 = (f32[256,64]{0,1:T(8,128)}, f32[256,64]{0,1:T(8,128)S(1)}, u32[]{:S(2)}) copy-start(f32[256,64]{0,1:T(8,128)S(1)} %get-tuple-element.101) | copy-start | bytes 196612
  127.5 83.7 %copy-start.45 = (f32[256,64]{0,1:T(8,128)}, f32[256,64]{0,1:T(8,128)S(1)}, u32[]{:S(2)}) copy-start(f32[256,64]{0,1:T(8,128)S(1)} %get-tuple-element.63) | copy-start | bytes 196612
  164.7 46.7 %copy-start.12 = (bf16[1024,320]{0,1:T(8,128)(2,1)}, bf16[1024,320]{0,1:T(8,128)(2,1)S(1)}, u32[]{:S(2)}) copy-start(bf16[1024,320]{0,1:T(8,128)(2,1)S(1)} %all-gather.1) | copy-start | bytes 1966084
  226.0 42.7 %copy-start.23 = (bf16[1024,320]{0,1:T(8,128)(2,1)S(1)}, bf16[1024,320]{0,1:T(8,128)(2,1)}, u32[]{:S(2)}) copy-start(bf16[1024,320]{0,1:T(8,128)(2,1)} %all-gather) | copy-start | bytes 1966084
  276.9 25.9 %copy-start.9 = (f32[256,960]{0,1:T(8,128)}, f32[256,960]{0,1:T(8,128)S(1)}, u32[]{:S(2)}) copy-start(f32[256,960]{0,1:T(8,128)S(1)} %get-tuple-element.88) | copy-start | bytes 2949124
  286.1 7.8 copy-start.22
  331.7 21.0 %copy-start.24 = (bf16[2,256,960]{1,2,0:T(8,128)(2,1)S(1)}, bf16[2,256,960]{1,2,0:T(8,128)(2,1)}, u32[]{:S(2)}) copy-start(bf16[2,256,960]{1,2,0:T(8,128)(2,1)} %param.25) | copy-start | bytes 2949124
  343.1 23.4 %slice-start.8 = ((s8[4915200]{0:T(1024)(128)(4,1)}), s8[720896]{0:T(1024)(128)(4,1)S(1)}, s32[]{:S(2)}) async-start(s8[4915200]{0:T(1024)(128)(4,1)} %bitcast.419), calls=%async_computation.28 | async-start | bytes 1441792
  352.7 13.8 %slice-start.9 = ((s8[4915200]{0:T(1024)(128)(4,1)}), s8[4194304]{0:T(1024)(128)(4,1)S(1)}, s32[]{:S(2)}) async-start(s8[4915200]{0:T(1024)(128)(4,1)} %bitcast.419), calls=%async_computation.29 | async-start | bytes 8388608
  361.6 8.1 slice-start.10
  377.0 8.0 slice-start.4
  394.1 8.2 copy-start.15
  410.8 13.1 %slice-start = ((s8[15728640]{0:T(1024)(128)(4,1)}), s8[4194304]{0:T(1024)(128)(4,1)S(1)}, s32[]{:S(2)}) async-start(s8[15728640]{0:T(1024)(128)(4,1)} %bitcast.415), calls=%async_computation.20 | async-start | bytes 8388608
  410.8 13.8 %slice-start.1 = ((s8[15728640]{0:T(1024)(128)(4,1)}), s8[4194304]{0:T(1024)(128)(4,1)S(1)}, s32[]{:S(2)}) async-start(s8[15728640]{0:T(1024)(128)(4,1)} %bitcast.415), calls=%async_computation.21 | async-start | bytes 8388608
  410.8 15.2 %slice-start.2 = ((s8[15728640]{0:T(1024)(128)(4,1)}), s8[4194304]{0:T(1024)(128)(4,1)S(1)}, s32[]{:S(2)}) async-start(s8[15728640]{0:T(1024)(128)(4,1)} %bitcast.415), calls=%async_computation.22 | async-start | bytes 8388608
  410.8 16.0 %slice-start.3 = ((s8[15728640]{0:T(1024)(128)(4,1)}), s8[3145728]{0:T(1024)(128)(4,1)S(1)}, s32[]{:S(2)}) async-start(s8[15728640]{0:T(1024)(128)(4,1)} %bitcast.415), calls=%async_computation.23 | async-start | bytes 6291456
  426.8 7.6 copy-start.13
  450.7 82.3 %all-to-all-start = ((bf16[8,4,28800]{2,0,1:T(8,128)(2,1)}), bf16[8,4,28800]{2,0,1:T(8,128)(2,1)}, u32[]{:S(2)}, u32[]{:S(2)}) async-start(bf16[8,4,28800]{2,0,1:T(8,128)(2,1)} %copy.55), calls=%async_computation.4 | async-start | bytes 3686400 | tf_op jit(solution)/shard_map/all_to_all | solution.py:102
  455.1 76.8 %reduce-scatter.5.cloned.1.call-start = ((), (), s32[]{:S(2)}) async-start(), calls=%async_computation.13 | async-start | bytes 819200 | tf_op jit(solution)/shard_map/reduce_scatter | solution.py:333
  466.1 102.1 %reduce-scatter.7.cloned.1.call-start = ((), (), s32[]{:S(2)}) async-start(), calls=%async_computation.14 | async-start | bytes 819200 | tf_op jit(solution)/shard_map/reduce_scatter | solution.py:339
  493.2 77.4 %reduce-scatter.11.cloned.1.call-start = ((), (), s32[]{:S(2)}) async-start(), calls=%async_computation.16 | async-start | bytes 819200 | tf_op jit(solution)/shard_map/reduce_scatter | solution.py:339
  493.5 9.1 copy-start.62
  533.0 31.0 %all-to-all-start.3 = ((bf16[8,4,28800]{2,0,1:T(8,128)(2,1)}), bf16[8,4,28800]{2,0,1:T(8,128)(2,1)}, u32[]{:S(2)}, u32[]{:S(2)}) async-start(bf16[8,4,28800]{2,0,1:T(8,128)(2,1)} %copy.60), calls=%async_computation.7 | async-start | bytes 3686400 | tf_op jit(solution)/shard_map/all_to_all | solution.py:111
  564.0 14.1 %all-to-all-start.1 = ((bf16[8,4,9600]{2,0,1:T(8,128)(2,1)}), bf16[8,4,9600]{2,0,1:T(8,128)(2,1)}, u32[]{:S(2)}, u32[]{:S(2)}) async-start(bf16[8,4,9600]{2,0,1:T(8,128)(2,1)} %copy.57), calls=%async_computation.5 | async-start | bytes 1228800 | tf_op jit(solution)/shard_map/all_to_all | solution.py:105
  578.1 19.9 %all-to-all-start.2 = ((bf16[8,4,9600]{2,0,1:T(8,128)(2,1)}), bf16[8,4,9600]{2,0,1:T(8,128)(2,1)S(1)}, u32[]{:S(2)}, u32[]{:S(2)}) async-start(bf16[8,4,9600]{2,0,1:T(8,128)(2,1)} %copy.59), calls=%async_computation.6 | async-start | bytes 1228800 | tf_op jit(solution)/shard_map/all_to_all | solution.py:108
  597.9 61.4 %all-to-all-start.4 = ((bf16[8,4,76800]{2,0,1:T(8,128)(2,1)}), bf16[8,4,76800]{2,0,1:T(8,128)(2,1)}, u32[]{:S(2)}, u32[]{:S(2)}) async-start(bf16[8,4,76800]{2,0,1:T(8,128)(2,1)} %copy.61), calls=%async_computation.8 | async-start | bytes 9830400 | tf_op jit(solution)/shard_map/all_to_all | solution.py:114
  617.7 67.0 %collective-permute-start.2 = (bf16[8,1,76800]{2,0,1:T(8,128)(2,1)}, bf16[8,1,76800]{2,0,1:T(8,128)(2,1)}, u32[]{:S(2)}, u32[]{:S(2)}) collective-permute-start(bf16[8,1,76800]{2,0,1:T(8,128)(2,1)} %bitcast.411), channel_id=1, source_target_pairs={{0,3},{1,2},{2,1},{3,0},{4,7},{5,6},{6,5},{7,4},{8,11},{9,10},{10,... | collective-permute-start | bytes 3686408 | tf_op jit(solution)/shard_map/ppermute | solution.py:34
  621.0 91.0 %collective-permute-start.1 = (bf16[8,1,76800]{2,0,1:T(8,128)(2,1)}, bf16[8,1,76800]{2,0,1:T(8,128)(2,1)}, u32[]{:S(2)}, u32[]{:S(2)}) collective-permute-start(bf16[8,1,76800]{2,0,1:T(8,128)(2,1)} %bitcast.412), channel_id=1, source_target_pairs={{0,2},{1,3},{2,0},{3,1},{4,6},{5,7},{6,4},{7,5},{8,10},{9,11},{10,... | collective-permute-start | bytes 3686408 | tf_op jit(solution)/shard_map/ppermute | solution.py:34
  622.8 89.2 %collective-permute-start = (bf16[8,1,76800]{2,0,1:T(8,128)(2,1)}, bf16[8,1,76800]{2,0,1:T(8,128)(2,1)}, u32[]{:S(2)}, u32[]{:S(2)}) collective-permute-start(bf16[8,1,76800]{2,0,1:T(8,128)(2,1)} %bitcast.413), channel_id=1, source_target_pairs={{0,1},{1,0},{2,3},{3,2},{4,5},{5,4},{6,7},{7,6},{8,9},{9,8},{10,11... | collective-permute-start | bytes 3686408 | tf_op jit(solution)/shard_map/ppermute | solution.py:34
  659.3 104.9 %all-to-all-start.5 = ((bf16[8,4,76800]{2,0,1:T(8,128)(2,1)}), bf16[8,4,76800]{2,0,1:T(8,128)(2,1)}, u32[]{:S(2)}, u32[]{:S(2)}) async-start(bf16[8,4,76800]{2,0,1:T(8,128)(2,1)} %copy.67), calls=%async_computation.9 | async-start | bytes 9830400 | tf_op jit(solution)/shard_map/all_to_all | solution.py:118
  664.3 281.5 %all-reduce.11.cloned.1.call-start = ((), (), s32[]{:S(2)}) async-start(), calls=%async_computation.19 | async-start | bytes 9830400
  784.1 47.9 %copy-start.6 = (f32[256,960]{0,1:T(8,128)S(1)}, f32[256,960]{0,1:T(8,128)}, u32[]{:S(2)}) copy-start(f32[256,960]{0,1:T(8,128)} %copy-done.5) | copy-start | bytes 2949124
  784.1 47.9 %copy-start.84 = (f32[256]{0:T(256)S(1)}, f32[256]{0:T(256)}, u32[]{:S(2)}) copy-start(f32[256]{0:T(256)} %get-tuple-element.73) | copy-start | bytes 3076
  784.1 47.9 %copy-start.85 = (f32[256]{0:T(256)S(1)}, f32[256]{0:T(256)}, u32[]{:S(2)}) copy-start(f32[256]{0:T(256)} %get-tuple-element.99) | copy-start | bytes 3076
  (76 other events, 218.7 us)
Sparse Core Ops, SparseCore 0:
  11.5 66.6 all-gather.19
  81.7 61.2 all-gather.21
  145.8 65.4 all-gather.13
  214.0 63.1 all-gather.15
  279.9 63.1 all-gather.17
  408.4 21.2 reduce-scatter.8
  466.2 22.5 reduce-scatter.4
  493.3 22.5 reduce-scatter.6
  524.5 26.0 reduce-scatter.10
  768.9 176.8 all-reduce.10
